TPU v7x, 32 devices: a whole 2x2x4 slice. The times are simulated.
32 devices in a mesh: seq: 8 (over z, y), head: 4 (over x, core).
Axes of the slice: x: 2, y: 2, z: 4, core: 2. Of those that a mesh axis runs over, the one named last changes fastest.
Arguments:
- tokens: bfloat16 [4096, 3072], P(('seq', 'head')), may hold values from -6 to 6
- owner_shard: int32 [4096, 1], P(('seq', 'head')), may hold values from 0 to 7; in each aligned block of 128 rows (0 to 127, 128 to 255, ...) at most 48 rows name the same one
- dest_slot: int32 [4096], P(('seq', 'head')), may hold values from 0 to 127
- w_qkv: bfloat16 [3072, 3, 1536], P(None, None, 'head'), may hold values from -0.109375 to 0.109375
- w_out: bfloat16 [1536, 3072], P('head'), may hold values from -3 to 3
- norm_gain: float32 [3072], replicated, may hold values from 0.5 to 1.5
- norm_shift: float32 [3072], replicated, may hold values from -3 to 3
- query_gain: float32 [128], replicated, may hold values from 0.5 to 16
- key_gain: float32 [128], replicated, may hold values from 0.5 to 16
- out_gate: float32 [3072], replicated, may hold values from 0.5 to 2
Outputs:
- unmerged: bfloat16 [4096, 3072], P(('seq', 'head'))
Inputs may be any that keep to these rules, and one draw needn't show every extreme that they name: `owner_shard`: among the rows of one device at most 48 name the same owner, a bound that some block reaches of them on some or all devices.
All inputs are finite; a program needn't handle non-finite values.
Results may differ from a plain program's by a relative error of at most 0.01195.
The roundings to bfloat16 on the way count: a program that leaves them out, or rounds other values in their place, can miss the bound.
Values may be sent and summed in bfloat16 or wider, within the bound.
A program may use at most 128 MiB of HBM per device.

v0:
```python
import math

import jax
import jax.numpy as jnp
from jax import lax
from jax.sharding import PartitionSpec as P

HDIM = 128
RATIO = 4


def rms_scale(values_in):
    return values_in * lax.rsqrt(jnp.mean(values_in * values_in, -1, keepdims=True) + 1e-06)


def normalize(merged_sums, norm_gain, norm_shift):
    row_mean = jnp.mean(merged_sums, -1, keepdims=True)
    centered = merged_sums - row_mean
    row_var = jnp.mean(centered * centered, -1, keepdims=True)
    return (centered * lax.rsqrt(row_var + 1e-06) * norm_gain + norm_shift).astype(jnp.bfloat16)


def on_device(
    tokens,
    owner_shard,
    dest_slot,
    w_qkv,
    w_out,
    norm_gain,
    norm_shift,
    query_gain,
    key_gain,
    out_gate,
):
    seq_count = lax.axis_size("seq")
    head_count = lax.axis_size("head")
    src_rows, feature_width = tokens.shape
    capacity = 3 * src_rows // seq_count
    merged_rows = src_rows * head_count // RATIO
    owners = owner_shard[:, 0]
    member = (owners[:, None] == jnp.arange(seq_count, dtype=jnp.int32)[None, :]).astype(jnp.int32)
    ranking = jnp.sum(member * (jnp.cumsum(member, 0) - 1), 1)
    position = owners * capacity + ranking
    packed = jnp.zeros((seq_count * capacity, feature_width), jnp.bfloat16).at[position].set(tokens)
    labels = jnp.full((seq_count * capacity,), -1, jnp.int32).at[position].set(dest_slot)
    arrived, arrived_ids = (
        lax.all_to_all(
            packed.reshape(seq_count, capacity, feature_width),
            "seq",
            split_axis=0,
            concat_axis=0,
            tiled=True,
        ),
        lax.all_to_all(
            labels.reshape(seq_count, capacity), "seq", split_axis=0, concat_axis=0, tiled=True
        ),
    )
    arrived = arrived.reshape(seq_count * capacity, feature_width)
    arrived_ids = arrived_ids.reshape(seq_count * capacity)
    selector = jnp.arange(merged_rows, dtype=jnp.int32)[:, None] == arrived_ids[None, :]
    partial_sums = jnp.dot(
        selector.astype(jnp.bfloat16), arrived, preferred_element_type=jnp.float32
    )
    total_sums = lax.psum(partial_sums, "head")
    normed = normalize(total_sums, norm_gain, norm_shift)
    head_width = w_qkv.shape[2]
    local_heads = head_width // HDIM
    projected = jnp.dot(
        normed, w_qkv.reshape(feature_width, 3 * head_width), preferred_element_type=jnp.float32
    )
    projected = projected.reshape(merged_rows, 3, local_heads, HDIM)
    queries = (rms_scale(projected[:, 0]) * query_gain / math.sqrt(HDIM)).astype(jnp.bfloat16)
    keys_local = (rms_scale(projected[:, 1]) * key_gain).astype(jnp.bfloat16)
    values_local = projected[:, 2].astype(jnp.bfloat16)
    weighted = jnp.zeros((merged_rows, local_heads, HDIM), jnp.float32)
    running_peak = jnp.full((local_heads, merged_rows), -jnp.inf, jnp.float32)
    running_total = jnp.zeros((local_heads, merged_rows), jnp.float32)
    key_block = lax.all_gather(
        keys_local.reshape(merged_rows, head_width), "seq", axis=0, tiled=True
    ).reshape(-1, local_heads, HDIM)
    value_block = lax.all_gather(
        values_local.reshape(merged_rows, head_width), "seq", axis=0, tiled=True
    ).reshape(-1, local_heads, HDIM)
    scores = jnp.einsum("qhd,khd->hqk", queries, key_block, preferred_element_type=jnp.float32)
    new_peak = jnp.max(scores, -1)
    rescale = jnp.exp(running_peak - new_peak)
    expweights = jnp.exp(scores - new_peak[:, :, None])
    running_total = running_total * rescale + jnp.sum(expweights, -1)
    update = jnp.einsum(
        "hqk,khd->qhd",
        expweights.astype(jnp.bfloat16),
        value_block,
        preferred_element_type=jnp.float32,
    )
    weighted = weighted * jnp.transpose(rescale)[:, :, None] + update
    weighted, running_peak, running_total = (weighted, new_peak, running_total)
    attended = (weighted / jnp.transpose(running_total)[:, :, None]).astype(jnp.bfloat16)
    attended = attended.reshape(merged_rows, head_width)
    summed_out = lax.psum(
        jnp.dot(attended, w_out, preferred_element_type=jnp.float32).astype(jnp.bfloat16), "head"
    ).astype(jnp.float32)
    merged_out = (summed_out * out_gate).astype(jnp.bfloat16)
    fetched = jnp.take(merged_out, jnp.maximum(arrived_ids, 0), axis=0)
    fetched = jnp.where(arrived_ids[:, None] >= 0, fetched, jnp.zeros_like(fetched))
    returned = lax.all_to_all(
        fetched.reshape(seq_count, capacity, feature_width),
        "seq",
        split_axis=0,
        concat_axis=0,
        tiled=True,
    )
    returned = returned.reshape(seq_count * capacity, feature_width)
    return jnp.take(returned, position, axis=0)


def solution(mesh):
    placed = (
        P(("seq", "head"), None),
        P(("seq", "head"), None),
        P(("seq", "head")),
        P(None, None, "head"),
        P("head", None),
        P(),
        P(),
        P(),
        P(),
        P(),
    )
    return jax.shard_map(
        on_device, mesh=mesh, in_specs=placed, out_specs=P(("seq", "head"), None), check_vma=False
    )
```

profile of v0, /device:TPU:25, one launch (start us, length us, event | category | flops | bytes accessed | tf_op | source)
XLA Modules:
  0.0 304.2 jit_solution(1108039326031762125)
XLA Ops:
  6.5 0.0 copy-start
  6.5 0.9 fusion.24
  7.4 0.2 reduce_window_sum.11
  7.6 0.8 select_reduce_fusion
  8.4 0.7 and_bitcast_fusion
  9.1 1.1 scatter_custom_fusion
  10.2 0.7 all_to_all.12
  10.9 5.5 %all-to-all-start = ((s32[8,1,48]{2,1,0:T(1,128)}), s32[8,1,48]{2,1,0:T(1,128)S(1)}, u32[]{:S(2)}, u32[]{:S(2)}) async-start(s32[8,1,48]{2,1,0:T(1,128)} %all_to_all.12), calls=%async_computation | async-start | bytes 8192 | tf_op jit(solution)/shard_map/all_to_all | solution.py:54
  16.4 4.0 %scatter_custom_fusion.1 = bf16[384,3072]{1,0:T(8,128)(2,1)} fusion(s32[128]{0:T(128)S(1)} %bitcast.86, bf16[128,3072]{1,0:T(8,128)(2,1)} %param.10, bf16[]{:T(256)} %constant.37.clone.1), kind=kCustom, calls=%fused_computation.12 | custom fusion | bytes 2359808 | tf_op jit(solution)/shard_map/scatter | solution.py:44
  20.4 0.0 all-to-all-done
  20.4 5.5 %all-to-all-start.1 = ((bf16[8,48,3072]{2,1,0:T(8,128)(2,1)}), bf16[8,48,3072]{2,1,0:T(8,128)(2,1)}, u32[]{:S(2)}, u32[]{:S(2)}) async-start(bf16[8,48,3072]{2,1,0:T(8,128)(2,1)} %bitcast.75), calls=%async_computation.1 | async-start | bytes 4718592 | tf_op jit(solution)/shard_map/all_to_all | solution.py:47
  25.9 0.0 all-reduce.3.cloned.1.call-start
  25.9 0.5 broadcast.157
  26.4 0.7 reduce.4
  27.1 0.1 reshape.128
  27.2 51.3 %all-to-all-done.1 = bf16[8,48,3072]{2,1,0:T(8,128)(2,1)} async-done(((bf16[8,48,3072]{2,1,0:T(8,128)(2,1)}), bf16[8,48,3072]{2,1,0:T(8,128)(2,1)}, u32[]{:S(2)}, u32[]{:S(2)}) %all-to-all-start.1) | async-done | bytes 2359328 | tf_op jit(solution)/shard_map/all_to_all | solution.py:47
  78.5 3.4 %fusion.18 = f32[128,3072]{1,0:T(8,128)} fusion(bf16[384,3072]{1,0:T(8,128)(2,1)} %bitcast.9, s32[384]{0:T(512)S(1)} %reshape.128), kind=kOutput, calls=%fused_computation.35 | convolution fusion | flops 302039040 | bytes 3933696 | tf_op jit(solution)/shard_map/dot_general | solution.py:61
  81.9 0.0 all-reduce.3.cloned.1.call-update
  82.0 0.0 copy-start.5
  82.0 0.0 all-reduce.5.cloned.1.call-start
  82.0 10.3 %copy.20 = bf16[3072,3,384]{0,2,1:T(8,128)(2,1)} copy(bf16[3072,3,384]{2,0,1:T(8,128)(2,1)} %param.13) | data formatting | bytes 14155776 | tf_op args[3]
  92.3 0.0 copy-done.5
  92.3 0.0 copy-start.3
  92.3 0.0 copy-start.4
  92.4 32.9 %all-reduce.3.cloned.1.call-done = f32[128,3072]{1,0:T(8,128)} async-done(((f32[128,3072]{1,0:T(8,128)}), f32[128,3072]{1,0:T(8,128)}) %all-reduce.3.cloned.1.call-update) | async-done | bytes 1572880 | tf_op jit(solution)/shard_map/psum | solution.py:64
  125.3 1.6 reduce_sum.60
  126.9 0.0 copy-start.1
  126.9 1.8 multiply_reduce_fusion
  128.7 0.0 copy-done.3
  128.7 0.0 copy-done.4
  128.7 0.0 copy-done.1
  128.7 5.1 %fusion.9 = f32[128,3,3,128]{0,3,2,1:T(8,128)S(1)} fusion(bf16[3,3,128,3072]{3,2,1,0:T(8,128)(2,1)} %bitcast.74, f32[128,3072]{1,0:T(8,128)S(1)} %copy-done.1, f32[3072]{0:T(1024)S(1)} %copy-done.3, f32[3072]{0:T(1024)S(1)} %copy-done.4, f32[128]{0:T(128)S(1)} %add_rsqrt_fusion.2, f32[128]{0:T(128)S(1)} %broadcast_multiply_fusion), kind=kOutput, calls=%fused_computation.19 | convolution fusion | flops 907935744 | bytes 9266176 | tf_op jit(solution)/shard_map/dot_general | solution.py:68
  133.9 0.0 copy-start.6
  134.0 0.1 fusion.17
  134.1 20.9 %all_gather.6 = bf16[1024,384]{0,1:T(8,128)(2,1)S(1)} all-gather(bf16[128,384]{0,1:T(8,128)(2,1)S(1)} %fusion.17), channel_id=1, replica_groups=mesh['seq'=8,'head'=4] {'seq'}, dimensions={0}, use_global_device_ids=true | all-gather | bytes 884736 | tf_op jit(solution)/shard_map/all_gather | solution.py:78
  155.1 0.0 copy-done.6
  155.1 0.6 fusion.28
  155.6 0.4 fusion
  156.0 25.7 %all_gather.7 = bf16[1024,384]{0,1:T(8,128)(2,1)S(1)} all-gather(bf16[128,384]{0,1:T(8,128)(2,1)S(1)} %bitcast.79), channel_id=1, replica_groups=mesh['seq'=8,'head'=4] {'seq'}, dimensions={0}, use_global_device_ids=true | all-gather | bytes 884736 | tf_op jit(solution)/shard_map/all_gather | solution.py:81
  181.7 0.5 fusion.6
  182.2 0.0 copy-done
  182.2 0.0 copy-start.2
  182.2 1.5 convolution_convert_fusion
  183.7 0.0 all-reduce.5.cloned.1.call-update
  183.7 0.1 reshape.138
  183.8 42.0 %all-reduce.5.cloned.1.call-done = bf16[128,3072]{1,0:T(8,128)(2,1)} async-done(((bf16[128,3072]{1,0:T(8,128)(2,1)}), bf16[128,3072]{1,0:T(8,128)(2,1)}) %all-reduce.5.cloned.1.call-update) | async-done | bytes 786448 | tf_op jit(solution)/shard_map/psum | solution.py:99
  225.9 0.0 copy-done.2
  225.9 1.3 multiply_convert_fusion
  227.2 3.6 %gather_fusion = bf16[384,3072]{1,0:T(8,128)(2,1)} fusion(bf16[128,3072]{1,0:T(8,128)(2,1)S(1)} %multiply_convert_fusion, s32[1024]{0:T(1024)S(1)} %pad_clamp_fusion.1), kind=kCustom, calls=%fused_computation | custom fusion | bytes 4720128 | tf_op jit(solution)/shard_map/jit(_take)/gather | solution.py:103
  230.7 3.4 %select_select_fusion = bf16[8,48,3072]{2,1,0:T(8,128)(2,1)} fusion(bf16[8,48,3072]{2,1,0:T(8,128)(2,1)} %bitcast.76, pred[8,48]{1,0:T(8,128)(4,1)S(1)} %get-tuple-element.10, pred[8,48]{1,0:T(8,128)(4,1)S(1)} %get-tuple-element.9), kind=kLoop, calls=%fused_computation.5 | loop fusion | flops 2359296 | bytes 4719360 | tf_op jit(solution)/shard_map/jit(_where)/select_n | solution.py:104
  234.2 5.4 %all-to-all-start.2 = ((bf16[8,48,3072]{2,1,0:T(8,128)(2,1)}), bf16[8,48,3072]{2,1,0:T(8,128)(2,1)}, u32[]{:S(2)}, u32[]{:S(2)}) async-start(bf16[8,48,3072]{2,1,0:T(8,128)(2,1)} %select_select_fusion), calls=%async_computation.2 | async-start | bytes 4718592 | tf_op jit(solution)/shard_map/all_to_all | solution.py:105
  239.6 52.9 %all-to-all-done.2 = bf16[8,48,3072]{2,1,0:T(8,128)(2,1)} async-done(((bf16[8,48,3072]{2,1,0:T(8,128)(2,1)}), bf16[8,48,3072]{2,1,0:T(8,128)(2,1)}, u32[]{:S(2)}, u32[]{:S(2)}) %all-to-all-start.2) | async-done | bytes 2359328 | tf_op jit(solution)/shard_map/all_to_all | solution.py:105
  292.5 3.8 %gather_fusion.1 = bf16[128,3072]{1,0:T(8,128)(2,1)S(1)} fusion(bf16[384,3072]{1,0:T(8,128)(2,1)} %bitcast.27, s32[1024]{0:T(1024)S(1)} %pad_clamp_fusion), kind=kCustom, calls=%fused_computation.1 | custom fusion | bytes 1573376 | tf_op jit(solution)/shard_map/jit(_take)/gather | solution.py:113
  296.3 1.0 broadcast_select_fusion
  (14 shorter events, 0.2 us)
Async XLA Ops:
  6.5 175.7 %copy-start = (bf16[384,3072]{1,0:T(8,128)(2,1)S(1)}, bf16[384,3072]{1,0:T(8,128)(2,1)}, u32[]{:S(2)}) copy-start(bf16[384,3072]{1,0:T(8,128)(2,1)} %param.14) | copy-start | bytes 7077892
  10.9 9.5 %all-to-all-start = ((s32[8,1,48]{2,1,0:T(1,128)}), s32[8,1,48]{2,1,0:T(1,128)S(1)}, u32[]{:S(2)}, u32[]{:S(2)}) async-start(s32[8,1,48]{2,1,0:T(1,128)} %all_to_all.12), calls=%async_computation | async-start | bytes 8192 | tf_op jit(solution)/shard_map/all_to_all | solution.py:54
  20.4 58.1 %all-to-all-start.1 = ((bf16[8,48,3072]{2,1,0:T(8,128)(2,1)}), bf16[8,48,3072]{2,1,0:T(8,128)(2,1)}, u32[]{:S(2)}, u32[]{:S(2)}) async-start(bf16[8,48,3072]{2,1,0:T(8,128)(2,1)} %bitcast.75), calls=%async_computation.1 | async-start | bytes 4718592 | tf_op jit(solution)/shard_map/all_to_all | solution.py:47
  25.9 99.4 %all-reduce.3.cloned.1.call-start = ((), (), s32[]{:S(2)}) async-start(), calls=%async_computation.3 | async-start | bytes 3145728 | tf_op jit(solution)/shard_map/psum | solution.py:64
  82.0 10.4 %copy-start.5 = (f32[128]{0:T(128)S(1)}, f32[128]{0:T(128)}, u32[]{:S(2)}) copy-start(f32[128]{0:T(128)} %param.18) | copy-start | bytes 1540
  82.0 143.9 %all-reduce.5.cloned.1.call-start = ((), (), s32[]{:S(2)}) async-start(), calls=%async_computation.4 | async-start | bytes 1572864 | tf_op jit(solution)/shard_map/psum | solution.py:99
  92.3 36.4 %copy-start.3 = (f32[3072]{0:T(1024)S(1)}, f32[3072]{0:T(1024)}, u32[]{:S(2)}) copy-start(f32[3072]{0:T(1024)} %param.16) | copy-start | bytes 36868
  92.3 36.4 %copy-start.4 = (f32[3072]{0:T(1024)S(1)}, f32[3072]{0:T(1024)}, u32[]{:S(2)}) copy-start(f32[3072]{0:T(1024)} %param.15) | copy-start | bytes 36868
  126.9 1.9 copy-start.1
  133.9 21.2 %copy-start.6 = (f32[128]{0:T(128)S(1)}, f32[128]{0:T(128)}, u32[]{:S(2)}) copy-start(f32[128]{0:T(128)} %param.17) | copy-start | bytes 1540
  182.2 43.7 %copy-start.2 = (f32[3072]{0:T(1024)S(1)}, f32[3072]{0:T(1024)}, u32[]{:S(2)}) copy-start(f32[3072]{0:T(1024)} %param.19) | copy-start | bytes 36868
  234.2 58.3 %all-to-all-start.2 = ((bf16[8,48,3072]{2,1,0:T(8,128)(2,1)}), bf16[8,48,3072]{2,1,0:T(8,128)(2,1)}, u32[]{:S(2)}, u32[]{:S(2)}) async-start(bf16[8,48,3072]{2,1,0:T(8,128)(2,1)} %select_select_fusion), calls=%async_computation.2 | async-start | bytes 4718592 | tf_op jit(solution)/shard_map/all_to_all | solution.py:105
Sparse Core Ops, SparseCore 0:
  82.1 43.1 all-reduce.2
  183.8 41.9 all-reduce.4
where the time goes:
time: 308 us; the launch traced here: 304 us
  waiting for transfers between devices  179 us (58%)
  blocking collectives  46.6 us (15%)
  local copies, waits for them, and re-layouts  24.2 us (8%)
  starting transfers between devices  16.5 us (5%)
  between operations  13.6 us (4%)
  other arithmetic  13 us (4%)
  matrix products  11.1 us (4%)
    all_to_all x1, waiting for transfers between devices, on_device(): lax.all_to_all(fetched.reshape(seq_count, capacity, feature_width), 'seq'...  52.9 us
    all_to_all x1, waiting for transfers between devices, on_device(): lax.all_to_all(packed.reshape(seq_count, capacity, feature_width), 'seq',...  51.3 us
    psum x1, waiting for transfers between devices, on_device(): lax.psum(jnp.dot(attended, w_out, preferred_element_type=jnp.float32).ast...  42 us
    psum x1, waiting for transfers between devices, on_device(): total_sums = lax.psum(partial_sums, 'head')  32.9 us
    all_gather x1, blocking collectives, on_device(): lax.all_gather(values_local.reshape(merged_rows, head_width), 'seq', axis...  25.7 us
    all_gather x1, blocking collectives, on_device(): lax.all_gather(keys_local.reshape(merged_rows, head_width), 'seq', axis=0...  20.9 us
    unnamed x15, local copies, waits for them, and re-layouts  10.4 us
  transfers between devices with their start and end apart: 5, of which 4 were waited for; matrix products, arithmetic and copies ran while one was open for 5% of the time, Pallas kernels for 0%

commit v1 on v0

v1 whole, which is shorter than its diff:
```python
import functools
import math

import jax
import jax.numpy as jnp
from jax import lax
from jax.experimental import pallas as pl
from jax.experimental.pallas import tpu as pltpu
from jax.sharding import PartitionSpec as P

HDIM = 128
RATIO = 4
MESH = pl.DeviceIdType.MESH
ANY = pl.BlockSpec(memory_space=pl.ANY)


def rms_scale(values_in):
    return values_in * lax.rsqrt(jnp.mean(values_in * values_in, -1, keepdims=True) + 1e-06)


def plane_width(seq_count):
    return 2 if seq_count % 2 == 0 else 1


class Plane:
    def __init__(self, seq_count, head_count):
        self.wide = plane_width(seq_count)
        self.heads = head_count
        self.size = self.wide * head_count

    def me(self):
        return lax.rem(lax.axis_index("seq"), self.wide) * self.heads + lax.axis_index("head")

    def device(self, index):
        base = lax.axis_index("seq") // self.wide * self.wide
        return (base + index // self.heads, lax.rem(index, self.heads))


class Line:
    def __init__(self, seq_count, head_count):
        self.wide = plane_width(seq_count)
        self.size = seq_count // self.wide

    def me(self):
        return lax.axis_index("seq") // self.wide

    def device(self, index):
        return (index * self.wide + lax.rem(lax.axis_index("seq"), self.wide), lax.axis_index("head"))


def greet(devices):
    barrier = pltpu.get_barrier_semaphore()
    for device in devices:
        pl.semaphore_signal(barrier, inc=1, device_id=device, device_id_type=MESH)
    pl.semaphore_wait(barrier, len(devices))


def exchange_kernel(group, count, source_of, target_of, *refs):
    sources, targets = refs[:count], refs[count : 2 * count]
    send_sem, recv_sem, own_sem = refs[2 * count :]
    size, me = group.size, group.me()
    others = [lax.rem(me + step, size) for step in range(1, size)]
    greet([group.device(other) for other in others])
    copies = []
    for step, other in enumerate(others):
        for item in range(count):
            copy = pltpu.make_async_remote_copy(
                src_ref=source_of[item](sources[item], other),
                dst_ref=target_of[item](targets[item], me),
                send_sem=send_sem.at[item, step],
                recv_sem=recv_sem.at[item, step],
                device_id=group.device(other),
                device_id_type=MESH,
            )
            copy.start()
            copies.append(copy)
    for item in range(count):
        own = pltpu.make_async_copy(
            source_of[item](sources[item], me), target_of[item](targets[item], me), own_sem.at[item]
        )
        own.start()
        copies.append(own)
    for copy in copies:
        copy.wait()


def exchange(number, group, arrays, shapes, source_of, target_of):
    count = len(arrays)
    return pl.pallas_call(
        functools.partial(exchange_kernel, group, count, source_of, target_of),
        out_shape=[
            jax.ShapeDtypeStruct(shape, array.dtype) for shape, array in zip(shapes, arrays)
        ],
        in_specs=[ANY] * count,
        out_specs=[ANY] * count,
        scratch_shapes=[
            pltpu.SemaphoreType.DMA((count, group.size - 1)),
            pltpu.SemaphoreType.DMA((count, group.size - 1)),
            pltpu.SemaphoreType.DMA((count,)),
        ],
        compiler_params=pltpu.CompilerParams(collective_id=number, has_side_effects=True),
        name="exchange_" + str(number),
    )(*arrays)


def whole(ref, index):
    return ref


def block(ref, index):
    return ref.at[index]


def columns(width, ref, index):
    return ref.at[:, pl.ds(pl.multiple_of(index * width, width), width)]


def gather_kernel(wide, length, count, *refs):
    sources, targets = refs[:count], refs[count : 2 * count]
    line_send, line_recv, side_send, side_recv, own_sem = refs[2 * count :]
    seq, head = lax.axis_index("seq"), lax.axis_index("head")
    z, y = seq // wide, lax.rem(seq, wide)
    beside = [z * wide + lax.rem(y + turn, wide) for turn in range(1, wide)]
    along = [lax.rem(z + step, length) for step in range(1, length)]
    greet([(z * wide + lax.rem(y + turn, wide), head) for turn in range(1, wide)]
          + [(other * wide + y, head) for other in along])
    copies, arriving = [], []

    def remote(source, target, send, recv, device):
        copy = pltpu.make_async_remote_copy(
            src_ref=source, dst_ref=target, send_sem=send, recv_sem=recv,
            device_id=device, device_id_type=MESH,
        )
        copy.start()
        return copy

    for step, other in enumerate(along):
        for item in range(count):
            arriving.append(remote(
                sources[item], targets[item].at[seq], line_send.at[item, step],
                line_recv.at[item, step], (other * wide + y, head)))
    for turn, other in enumerate(beside):
        for item in range(count):
            copies.append(remote(
                sources[item], targets[item].at[seq], side_send.at[item, turn, 0],
                side_recv.at[item, turn, 0], (other, head)))
    for item in range(count):
        own = pltpu.make_async_copy(sources[item], targets[item].at[seq], own_sem.at[item])
        own.start()
        copies.append(own)
    for step in range(length - 1):
        come = lax.rem(z + length - 1 - step, length) * wide + y
        for item in range(count):
            arriving[step * count + item].wait_recv()
            for turn, other in enumerate(beside):
                copies.append(remote(
                    targets[item].at[come], targets[item].at[come],
                    side_send.at[item, turn, step + 1], side_recv.at[item, turn, step + 1],
                    (other, head)))
    for copy in arriving:
        copy.wait_send()
    for copy in copies:
        copy.wait()


def gather_seq(number, seq_count, arrays):
    wide = plane_width(seq_count)
    length, count = seq_count // wide, len(arrays)
    return pl.pallas_call(
        functools.partial(gather_kernel, wide, length, count),
        out_shape=[jax.ShapeDtypeStruct((seq_count, *a.shape), a.dtype) for a in arrays],
        in_specs=[ANY] * count,
        out_specs=[ANY] * count,
        scratch_shapes=[
            pltpu.SemaphoreType.DMA((count, length)),
            pltpu.SemaphoreType.DMA((count, length)),
            pltpu.SemaphoreType.DMA((count, wide, length)),
            pltpu.SemaphoreType.DMA((count, wide, length)),
            pltpu.SemaphoreType.DMA((count,)),
        ],
        compiler_params=pltpu.CompilerParams(collective_id=number, has_side_effects=True),
        name="gather_" + str(number),
    )(*arrays)


def on_device(
    tokens,
    owner_shard,
    dest_slot,
    w_qkv,
    w_out,
    norm_gain,
    norm_shift,
    query_gain,
    key_gain,
    out_gate,
):
    seq_count = lax.axis_size("seq")
    head_count = lax.axis_size("head")
    src_rows, feature_width = tokens.shape
    merged_rows = src_rows * head_count // RATIO
    plane, line = Plane(seq_count, head_count), Line(seq_count, head_count)
    wide = plane.wide
    part = feature_width // plane.size
    own_columns = functools.partial(columns, part)
    first_column = plane.me() * part
    plane_tokens = plane.size * src_rows
    plane_rows = wide * merged_rows

    destination = (owner_shard[:, 0] * merged_rows + dest_slot)[None, :]
    seen, seen_ids = exchange(
        0,
        plane,
        [tokens, destination],
        [(plane.size, src_rows, part), (plane.size, 1, src_rows)],
        [own_columns, whole],
        [block, block],
    )
    seen = seen.reshape(plane_tokens, part)
    seen_ids = seen_ids.reshape(plane_tokens)
    selector = jnp.arange(seq_count * merged_rows, dtype=jnp.int32)[:, None] == seen_ids[None, :]
    partial_sums = jnp.dot(selector.astype(jnp.bfloat16), seen, preferred_element_type=jnp.float32)
    [gathered] = exchange(
        1,
        line,
        [partial_sums.reshape(line.size, plane_rows, part)],
        [(line.size, plane_rows, part)],
        [block],
        [block],
    )
    sums = jnp.sum(gathered, 0)
    part_mean = jnp.mean(sums, -1)
    part_spread = jnp.sum((sums - part_mean[:, None]) ** 2, -1)
    [stats] = exchange(
        2,
        plane,
        [jnp.stack([part_mean, part_spread])],
        [(plane.size, 2, plane_rows)],
        [whole],
        [block],
    )
    row_mean = jnp.mean(stats[:, 0], 0)
    apart = stats[:, 0] - row_mean[None, :]
    row_var = (jnp.sum(stats[:, 1], 0) + part * jnp.sum(apart * apart, 0)) / feature_width

    def own_part(vector):
        return lax.dynamic_slice(vector, (first_column,), (part,))

    normed = (
        (sums - row_mean[:, None]) * lax.rsqrt(row_var + 1e-06)[:, None] * own_part(norm_gain)
        + own_part(norm_shift)
    ).astype(jnp.bfloat16)
    [normed] = exchange(
        3,
        plane,
        [normed.reshape(wide, merged_rows, part)],
        [(merged_rows, feature_width)],
        [lambda ref, index: ref.at[index // head_count]],
        [own_columns],
    )
    head_width = w_qkv.shape[2]
    local_heads = head_width // HDIM
    weights = jnp.transpose(w_qkv, (1, 0, 2))

    def projected(which):
        return jnp.dot(normed, weights[which], preferred_element_type=jnp.float32)

    def by_head(values_in):
        return values_in.reshape(merged_rows, local_heads, HDIM)

    queries = (rms_scale(by_head(projected(0))) * query_gain / math.sqrt(HDIM)).astype(jnp.bfloat16)
    keys_local = (rms_scale(by_head(projected(1))) * key_gain).astype(jnp.bfloat16)
    values_local = projected(2).astype(jnp.bfloat16)
    keys_all, values_all = gather_seq(
        4,
        seq_count,
        [keys_local.reshape(merged_rows, head_width), values_local],
    )
    keys_all = keys_all.reshape(-1, local_heads, HDIM)
    values_all = values_all.reshape(-1, local_heads, HDIM)
    scores = jnp.einsum("qhd,khd->hqk", queries, keys_all, preferred_element_type=jnp.float32)
    expweights = jnp.exp(scores - jnp.max(scores, -1, keepdims=True))
    total = jnp.sum(expweights, -1)
    weighted = jnp.einsum(
        "hqk,khd->qhd",
        expweights.astype(jnp.bfloat16),
        values_all,
        preferred_element_type=jnp.float32,
    )
    attended = (weighted / jnp.transpose(total)[:, :, None]).astype(jnp.bfloat16)
    attended = attended.reshape(merged_rows, head_width)
    partial_out = jnp.dot(attended, w_out, preferred_element_type=jnp.float32).astype(jnp.bfloat16)
    [pieces] = exchange(
        5,
        plane,
        [partial_out],
        [(plane.size, merged_rows, part)],
        [own_columns],
        [block],
    )
    pieces = pieces.reshape(wide, head_count, merged_rows, part).astype(jnp.float32)
    merged_out = (jnp.sum(pieces, 1) * own_part(out_gate)).astype(jnp.bfloat16)
    [merged_all] = exchange(
        6,
        line,
        [merged_out.reshape(plane_rows, part)],
        [(line.size, plane_rows, part)],
        [whole],
        [block],
    )
    merged_all = merged_all.reshape(seq_count * merged_rows, part)
    chooser = seen_ids[:, None] == jnp.arange(seq_count * merged_rows, dtype=jnp.int32)[None, :]
    fetched = jnp.dot(
        chooser.astype(jnp.bfloat16), merged_all, preferred_element_type=jnp.float32
    ).astype(jnp.bfloat16)
    [returned] = exchange(
        7,
        plane,
        [fetched.reshape(plane.size, src_rows, part)],
        [(src_rows, feature_width)],
        [block],
        [own_columns],
    )
    return returned


def solution(mesh):
    placed = (
        P(("seq", "head"), None),
        P(("seq", "head"), None),
        P(("seq", "head")),
        P(None, None, "head"),
        P("head", None),
        P(),
        P(),
        P(),
        P(),
        P(),
    )
    return jax.shard_map(
        on_device, mesh=mesh, in_specs=placed, out_specs=P(("seq", "head"), None), check_vma=False
    )
```

time: 308 us -> 200 us (0.65)
  waiting for transfers between devices: 179 us -> 0 us
  Pallas kernels: 0 us -> 142 us
  blocking collectives: 46.6 us -> 0 us
  starting transfers between devices: 16.5 us -> 0 us
  between operations: 13.6 us -> 0.2 us
  matrix products: 11.1 us -> 22.5 us
  other arithmetic: 13 us -> 6.68 us
  local copies, waits for them, and re-layouts: 24.2 us -> 27.4 us
    pallas_call x0 -> x8, Pallas kernels: none -> 142 us  [the longest x7 113 us: exchange(): pl.pallas_call(functools.partial(exchange_kernel, group, count, source_of...]
    all_to_all x3 -> x0, waiting for transfers between devices: 104 us -> none  [the longest x1 52.9 us: on_device(): lax.all_to_all(fetched.reshape(seq_count, capacity, feature_width), 'seq'...]
    psum x2 -> x0, waiting for transfers between devices: 75 us -> none  [the longest x1 42 us: on_device(): lax.psum(jnp.dot(attended, w_out, preferred_element_type=jnp.float32).ast...]
    all_gather x2 -> x0, blocking collectives: 46.6 us -> none  [the longest x1 25.7 us: on_device(): lax.all_gather(values_local.reshape(merged_rows, head_width), 'seq', axis...]
    all_to_all x3 -> x0, starting transfers between devices: 16.4 us -> none  [the longest x1 5.49 us: on_device(): lax.all_to_all(labels.reshape(seq_count, capacity), 'seq', split_axis=0,...]
    dot_general x0 -> x3, local copies, waits for them, and re-layouts: none -> 13.7 us  [projected(): return jnp.dot(normed, weights[which], preferred_element_type=jnp.float32)]
    dot_general x4 -> x7, matrix products: 9.61 us -> 19.3 us  [the longest x3 8.17 us: projected(): return jnp.dot(normed, weights[which], preferred_element_type=jnp.float32)]
    unnamed x15 -> x21, local copies, waits for them, and re-layouts: 10.4 us -> 2.75 us
  transfers between devices with their start and end apart: 5 -> 0, of which waited for: 4 -> 0; matrix products, arithmetic and copies ran while one was open for 5% -> 0% of each run, Pallas kernels for 0% -> 0%
where the time goes in v1:
time: 200 us; the launch traced here: 199 us
  Pallas kernels  142 us (71%)
  local copies, waits for them, and re-layouts  27.4 us (14%)
  matrix products  22.5 us (11%)
  other arithmetic  6.68 us (3%)
    pallas_call x7, Pallas kernels, exchange(): pl.pallas_call(functools.partial(exchange_kernel, group, count, source_of...  113 us
    pallas_call x1, Pallas kernels, gather_seq(): pl.pallas_call(functools.partial(gather_kernel, wide, length, count), out...  29.8 us
    dot_general x3, local copies, waits for them, and re-layouts, projected(): return jnp.dot(normed, weights[which], preferred_element_type=jnp.float32)  13.7 us
    dot_general x3, matrix products, projected(): return jnp.dot(normed, weights[which], preferred_element_type=jnp.float32)  8.17 us

profile of v1, /device:TPU:25, one launch (start us, length us, event | category | flops | bytes accessed | tf_op | source)
XLA Modules:
  0.0 199.1 jit_solution(16344227513125456985)
XLA Ops:
  0.0 0.0 copy-start
  0.0 5.1 %slice_bitcast_fusion = (bf16[384,3072]{0,1:T(8,128)(2,1)}, bf16[384,3072]{0,1:T(8,128)(2,1)}) fusion(bf16[3,3072,384]{2,1,0:T(8,128)(2,1)} %bitcast.80), kind=kLoop, calls=%fused_computation.6 | loop fusion | bytes 9437184 | tf_op jit(solution)/shard_map/dot_general | solution.py:266
  5.2 0.0 copy-start.8
  5.2 0.0 copy-start.9
  5.2 4.3 %copy.17 = bf16[384,3072]{1,0:T(8,128)(2,1)} copy(bf16[384,3072]{0,1:T(8,128)(2,1)} %get-tuple-element.18) | data formatting | bytes 4718592 | tf_op jit(solution)/shard_map/dot_general | solution.py:266
  9.4 0.0 copy-done.8
  9.5 0.0 copy-done.9
  9.5 0.5 fusion.29.refs_1_
  10.0 13.1 %exchange_0.1 = (bf16[8,128,384]{2,1,0:T(8,128)(2,1)}, s32[8,1,128]{2,1,0:T(1,128)}) custom-call(bf16[128,3072]{1,0:T(8,128)(2,1)} %refs_0_.1, s32[1,128]{1,0:T(1,128)} %fusion.29.refs_1_), custom_call_target="tpu_custom_call" | custom-call | tf_op jit(solution)/shard_map/exchange_0/pallas_call | solution.py:89
  23.1 3.6 %fusion.2.refs_0_ = f32[4,256,384]{2,1,0:T(8,128)} fusion(bf16[1024,384,1]{1,0,2:T(8,128)(2,1)} %bitcast.88, s32[1024]{0:T(1024)} %bitcast.89, s32[4,256]{1,0:T(4,128)S(1)} %multiply_add_fusion), kind=kOutput, calls=%fused_computation.3 | convolution fusion | flops 806354944 | bytes 2367488 | tf_op jit(solution)/shard_map/dot_general | solution.py:222
  26.7 37.6 %exchange_1.1 = f32[4,256,384]{2,1,0:T(8,128)} custom-call(f32[4,256,384]{2,1,0:T(8,128)} %fusion.2.refs_0_), custom_call_target="tpu_custom_call" | custom-call | tf_op jit(solution)/shard_map/exchange_1/pallas_call | solution.py:89
  64.4 1.6 fusion.35
  66.0 0.8 dynamic_slice.10
  66.8 0.8 dynamic_slice.9
  67.6 0.2 multiply_reduce_fusion
  67.8 0.6 pad_maximum_fusion.refs_0_
  68.4 5.0 %exchange_2.1 = f32[8,2,256]{2,1,0:T(2,128)} custom-call(f32[2,256]{1,0:T(2,128)} %pad_maximum_fusion.refs_0_), custom_call_target="tpu_custom_call" | custom-call | tf_op jit(solution)/shard_map/exchange_2/pallas_call | solution.py:89
  73.4 0.8 slice_reduce_fusion.1
  74.2 0.0 copy-start.5
  74.2 0.8 add_convert_fusion.refs_0_
  75.1 11.8 %exchange_3.1 = bf16[128,3072]{1,0:T(8,128)(2,1)} custom-call(bf16[2,128,384]{2,1,0:T(8,128)(2,1)} %add_convert_fusion.refs_0_), custom_call_target="tpu_custom_call" | custom-call | tf_op jit(solution)/shard_map/exchange_3/pallas_call | solution.py:89
  86.9 0.0 copy-start.1
  86.9 2.8 %multiply_reduce_fusion.2 = (f32[128,3]{0,1:T(4,128)S(1)}, f32[128,3,128]{0,2,1:T(8,128)S(1)}) fusion(bf16[3,128,3072]{2,1,0:T(8,128)(2,1)} %bitcast.77, bf16[128,3072]{1,0:T(8,128)(2,1)} %exchange_3.1), kind=kOutput, calls=%fused_computation.35 | convolution fusion | flops 302087808 | bytes 3343872 | tf_op jit(solution)/shard_map/dot_general | solution.py:266
  89.7 0.0 copy-done.5
  89.7 0.1 multiply_convert_fusion.1
  89.8 0.8 copy.18.refs_0_
  90.5 0.0 copy-done.1
  90.5 2.9 %fusion.13.refs_1_ = bf16[128,384]{1,0:T(8,128)(2,1)} fusion(bf16[128,3072]{1,0:T(8,128)(2,1)S(1)} %copy-done.1, bf16[3,3072,384]{2,1,0:T(8,128)(2,1)} %bitcast.81), kind=kOutput, calls=%fused_computation.20 | convolution fusion | flops 302039040 | bytes 3244032 | tf_op jit(solution)/shard_map/dot_general | solution.py:266
  93.4 29.8 %gather_4.1 = (bf16[8,128,384]{2,1,0:T(8,128)(2,1)}, bf16[8,128,384]{2,1,0:T(8,128)(2,1)}) custom-call(bf16[128,384]{1,0:T(8,128)(2,1)} %copy.18.refs_0_, bf16[128,384]{1,0:T(8,128)(2,1)} %fusion.13.refs_1_), custom_call_target="tpu_custom_call" | custom-call | tf_op jit(solution)/shard_map/gather_4/pallas_call | solution.py:169
  123.2 2.5 %copy.19 = bf16[8,128,384]{1,0,2:T(8,128)(2,1)} copy(bf16[8,128,384]{2,1,0:T(8,128)(2,1)} %get-tuple-element.11) | data formatting | bytes 1572864 | tf_op jit(solution)/shard_map/gather_4/pallas_call | solution.py:169
  125.6 2.2 %reshape.139 = bf16[1024,3,128]{0,2,1:T(8,128)(2,1)} reshape(bf16[8,128,384]{1,0,2:T(8,128)(2,1)} %copy.19) | data formatting | bytes 1572864 | tf_op jit(solution)/shard_map/reshape | solution.py:280
  127.8 3.3 %reshape.148 = bf16[1024,3,128]{2,1,0:T(4,128)(2,1)} reshape(bf16[8,128,384]{2,1,0:T(8,128)(2,1)} %get-tuple-element.12) | data formatting | bytes 1572864 | tf_op jit(solution)/shard_map/reshape | solution.py:279
  131.0 4.3 %copy.20 = bf16[384,3072]{1,0:T(8,128)(2,1)} copy(bf16[384,3072]{0,1:T(8,128)(2,1)} %get-tuple-element.17) | data formatting | bytes 4718592 | tf_op jit(solution)/shard_map/dot_general | solution.py:266
  135.3 0.0 copy-start.2
  135.3 0.0 copy-start.6
  135.3 2.5 %multiply_reduce_fusion.1 = (f32[128,3]{0,1:T(4,128)S(1)}, f32[128,3,128]{0,2,1:T(8,128)S(1)}) fusion(bf16[3,128,3072]{2,1,0:T(8,128)(2,1)} %bitcast.78, bf16[128,3072]{1,0:T(8,128)(2,1)S(1)} %copy-done.1), kind=kOutput, calls=%fused_computation.33 | convolution fusion | flops 302087808 | bytes 3343872 | tf_op jit(solution)/shard_map/dot_general | solution.py:266
  137.8 0.0 copy-start.4
  137.8 0.0 copy-start.3
  137.9 0.6 copy-done.4
  138.5 0.0 copy-done.2
  138.5 0.0 copy-done.6
  138.5 1.6 fusion.14
  140.2 0.0 copy-done.3
  140.2 1.6 fusion.36
  141.8 2.6 %fusion.12 = bf16[128,3,128]{0,2,1:T(8,128)(2,1)S(1)} fusion(bf16[1024,3,128]{0,2,1:T(8,128)(2,1)} %reshape.139, f32[3,128,1024]{2,1,0:T(8,128)} %fusion.14, f32[128,3]{0,1:T(4,128)S(1)} %bitcast.91), kind=kOutput, calls=%fused_computation.19 | convolution fusion | flops 101549440 | bytes 2459136 | tf_op jit(solution)/shard_map/hqk,khd->qhd/dot_general | solution.py:284
  144.4 0.0 copy-done
  144.4 1.5 convolution_convert_fusion.refs_0_
  145.9 0.0 copy-start.7
  145.9 12.5 %exchange_5.1 = bf16[8,128,384]{2,1,0:T(8,128)(2,1)} custom-call(bf16[128,3072]{1,0:T(8,128)(2,1)} %convolution_convert_fusion.refs_0_), custom_call_target="tpu_custom_call" | custom-call | tf_op jit(solution)/shard_map/exchange_5/pallas_call | solution.py:89
  158.4 1.3 convert_reduce_fusion
  159.7 0.8 dynamic_slice.11
  160.4 0.7 fusion.21.refs_0_
  161.1 20.0 %exchange_6.1 = bf16[4,256,384]{2,1,0:T(8,128)(2,1)} custom-call(bf16[256,384]{1,0:T(8,128)(2,1)} %fusion.21.refs_0_), custom_call_target="tpu_custom_call" | custom-call | tf_op jit(solution)/shard_map/exchange_6/pallas_call | solution.py:89
  181.2 0.0 copy-done.7
  181.2 3.3 %fusion.10 = bf16[1024,384]{1,0:T(8,128)(2,1)} fusion(bf16[1024,384]{1,0:T(8,128)(2,1)} %bitcast.83, s32[1024]{0:T(1024)S(1)} %bitcast.90), kind=kOutput, calls=%fused_computation.16 | convolution fusion | flops 806748160 | bytes 1576960 | tf_op jit(solution)/shard_map/dot_general | solution.py:313
  184.5 12.5 %exchange_7.1 = bf16[128,3072]{1,0:T(8,128)(2,1)} custom-call(bf16[8,128,384]{2,1,0:T(8,128)(2,1)} %bitcast.82), custom_call_target="tpu_custom_call" | custom-call | tf_op jit(solution)/shard_map/exchange_7/pallas_call | solution.py:89
  197.0 2.1 %copy.38 = bf16[128,3072]{1,0:T(8,128)(2,1)} copy(bf16[128,3072]{1,0:T(8,128)(2,1)} %exchange_7.1) | data formatting | bytes 1572864
  (7 shorter events, 0.1 us)
Async XLA Ops:
  0.0 144.4 %copy-start = (bf16[384,3072]{1,0:T(8,128)(2,1)S(1)}, bf16[384,3072]{1,0:T(8,128)(2,1)}, u32[]{:S(2)}) copy-start(bf16[384,3072]{1,0:T(8,128)(2,1)} %param.14) | copy-start | bytes 7077892
  5.2 4.3 %copy-start.8 = (s32[128]{0:T(128)S(1)}, s32[128]{0:T(128)}, u32[]{:S(2)}) copy-start(s32[128]{0:T(128)} %param.12) | copy-start | bytes 1540
  5.2 4.3 %copy-start.9 = (s32[128,1]{0,1:T(1,128)S(1)}, s32[128,1]{0,1:T(1,128)}, u32[]{:S(2)}) copy-start(s32[128,1]{0,1:T(1,128)} %param.11) | copy-start | bytes 1540
  74.2 15.4 %copy-start.5 = (f32[128]{0:T(128)S(1)}, f32[128]{0:T(128)}, u32[]{:S(2)}) copy-start(f32[128]{0:T(128)} %param.18) | copy-start | bytes 1540
  86.9 3.6 %copy-start.1 = (bf16[128,3072]{1,0:T(8,128)(2,1)S(1)}, bf16[128,3072]{1,0:T(8,128)(2,1)}, u32[]{:S(2)}) copy-start(bf16[128,3072]{1,0:T(8,128)(2,1)} %exchange_3.1) | copy-start | bytes 2359300
  135.3 3.2 %copy-start.2 = (bf16[1024,3,128]{2,1,0:T(4,128)(2,1)S(1)}, bf16[1024,3,128]{2,1,0:T(4,128)(2,1)}, u32[]{:S(2)}) copy-start(bf16[1024,3,128]{2,1,0:T(4,128)(2,1)} %reshape.148) | copy-start | bytes 2359300
  135.3 3.2 %copy-start.6 = (f32[128]{0:T(128)S(1)}, f32[128]{0:T(128)}, u32[]{:S(2)}) copy-start(f32[128]{0:T(128)} %param.17) | copy-start | bytes 1540
  137.8 0.7 copy-start.4
  137.8 2.3 %copy-start.3 = (bf16[1024,3,128]{2,1,0:T(4,128)(2,1)S(1)}, bf16[1024,3,128]{2,1,0:T(4,128)(2,1)}, u32[]{:S(2)}) copy-start(bf16[1024,3,128]{2,1,0:T(4,128)(2,1)} %reshape.148) | copy-start | bytes 2359300
  145.9 35.2 %copy-start.7 = (s32[8,1,128]{2,1,0:T(1,128)S(1)}, s32[8,1,128]{2,1,0:T(1,128)}, u32[]{:S(2)}) copy-start(s32[8,1,128]{2,1,0:T(1,128)} %get-tuple-element.9) | copy-start | bytes 12292

commit v2 on v1

--- a/solution.py
+++ b/solution.py
@@ -116,7 +116,7 @@
 
 
 def gather_kernel(wide, length, count, *refs):
-    sources, targets = refs[:count], refs[count : 2 * count]
+    sources, targets = [ref.at[pl.ds(1, 2)] for ref in refs[:count]], refs[count : 2 * count]
     line_send, line_recv, side_send, side_recv, own_sem = refs[2 * count :]
     seq, head = lax.axis_index("seq"), lax.axis_index("head")
     z, y = seq // wide, lax.rem(seq, wide)
@@ -126,22 +126,19 @@
           + [(other * wide + y, head) for other in along])
     copies, arriving = [], []
 
-    def remote(source, target, send, recv, device):
-        copy = pltpu.make_async_remote_copy(
-            src_ref=source, dst_ref=target, send_sem=send, recv_sem=recv,
-            device_id=device, device_id_type=MESH,
-        )
+    def begin(*ends):
+        copy = remote(*ends)
         copy.start()
         return copy
 
     for step, other in enumerate(along):
         for item in range(count):
-            arriving.append(remote(
+            arriving.append(begin(
                 sources[item], targets[item].at[seq], line_send.at[item, step],
                 line_recv.at[item, step], (other * wide + y, head)))
     for turn, other in enumerate(beside):
         for item in range(count):
-            copies.append(remote(
+            copies.append(begin(
                 sources[item], targets[item].at[seq], side_send.at[item, turn, 0],
                 side_recv.at[item, turn, 0], (other, head)))
     for item in range(count):
@@ -153,7 +150,7 @@
         for item in range(count):
             arriving[step * count + item].wait_recv()
             for turn, other in enumerate(beside):
-                copies.append(remote(
+                copies.append(begin(
                     targets[item].at[come], targets[item].at[come],
                     side_send.at[item, turn, step + 1], side_recv.at[item, turn, step + 1],
                     (other, head)))
@@ -168,7 +165,7 @@
     length, count = seq_count // wide, len(arrays)
     return pl.pallas_call(
         functools.partial(gather_kernel, wide, length, count),
-        out_shape=[jax.ShapeDtypeStruct((seq_count, *a.shape), a.dtype) for a in arrays],
+        out_shape=[jax.ShapeDtypeStruct((seq_count, 2, *a.shape[1:]), a.dtype) for a in arrays],
         in_specs=[ANY] * count,
         out_specs=[ANY] * count,
         scratch_shapes=[
@@ -181,6 +178,266 @@
         compiler_params=pltpu.CompilerParams(collective_id=number, has_side_effects=True),
         name="gather_" + str(number),
     )(*arrays)
+
+
+LANES = 128
+VMEM = pl.BlockSpec(memory_space=pltpu.VMEM)
+
+
+def remote(source, target, send, recv, device):
+    return pltpu.make_async_remote_copy(
+        src_ref=source, dst_ref=target, send_sem=send, recv_sem=recv,
+        device_id=device, device_id_type=MESH,
+    )
+
+
+def to_row(column):
+    return jnp.transpose(jnp.broadcast_to(column, (column.shape[0], LANES)))[:8]
+
+
+def to_column(row):
+    return jnp.transpose(jnp.broadcast_to(row, (LANES, row.shape[1])))[:, :1]
+
+
+def front_kernel(
+    plane, line, chunks, tokens, ids, gain, shift, normed, all_ids, seen, part, passing, sums,
+    stats, parts, id_send, id_recv, seen_send, seen_recv, pass_send, pass_recv, stat_send,
+    stat_recv, norm_send, norm_recv, own_sem,
+):
+    me, z, length = plane.me(), line.me(), line.size
+    src_rows = tokens.shape[0]
+    rows = part.shape[2]
+    width = chunks * LANES
+    feature_width = width * plane.size
+    others = [lax.rem(me + step, plane.size) for step in range(1, plane.size)]
+    devices = [plane.device(other) for other in others]
+    above, below = lax.rem(z + 1, length), lax.rem(z + length - 1, length)
+    along = [lax.rem(z + step, length) for step in range(1, length)]
+    greet(devices + [line.device(other) for other in along])
+
+    def slab(index, chunk):
+        return pl.ds(pl.multiple_of(index * width + chunk * LANES, LANES), LANES)
+
+    started = []
+
+    def go(copy):
+        copy.start()
+        started.append(copy)
+        return copy
+
+    id_copies = [
+        go(remote(ids, all_ids.at[me], id_send.at[step], id_recv.at[step], device))
+        for step, device in enumerate(devices)
+    ]
+    seen_copies = [
+        [
+            go(remote(tokens.at[:, slab(other, chunk)], seen.at[chunk, me],
+                      seen_send.at[chunk, step], seen_recv.at[chunk, step], devices[step]))
+            for step, other in enumerate(others)
+        ]
+        for chunk in range(chunks)
+    ]
+    all_ids[me] = ids[...]
+    for chunk in range(chunks):
+        seen[chunk, me] = tokens[:, slab(me, chunk)]
+    for copy in id_copies:
+        copy.wait_recv()
+    labels = jnp.concatenate([all_ids[index] for index in range(plane.size)], axis=1)
+    places = lax.broadcasted_iota(jnp.int32, (rows, 1), 0)
+
+    def upward(chunk, dest):
+        return remote(part.at[chunk, dest], passing.at[chunk, dest + 1], pass_send.at[chunk, dest + 1],
+                      pass_recv.at[chunk, dest + 1], line.device(above))
+
+    def downward(chunk, dest):
+        return remote(part.at[chunk, dest], passing.at[chunk, dest], pass_send.at[chunk, dest],
+                      pass_recv.at[chunk, dest], line.device(below))
+
+    for chunk in range(chunks):
+        for copy in seen_copies[chunk]:
+            copy.wait_recv()
+        arrived = seen[chunk].reshape(plane.size * src_rows, LANES)
+        for dest in range(length):
+            chosen = (places + dest * rows == labels).astype(jnp.float32).astype(jnp.bfloat16)
+            part[chunk, dest] = jnp.dot(chosen, arrived, preferred_element_type=jnp.float32)
+        for turn in range(length - 1):
+            high, low = length - 1 - turn, turn
+
+            @pl.when(z < high)
+            def _():
+                @pl.when(z > 0)
+                def _():
+                    upward(chunk, high).wait_recv()
+                    part[chunk, high] += passing[chunk, high + 1]
+                upward(chunk, high).start()
+
+            @pl.when(z > low)
+            def _():
+                @pl.when(z < length - 1)
+                def _():
+                    downward(chunk, low).wait_recv()
+                    part[chunk, low] += passing[chunk, low]
+                downward(chunk, low).start()
+
+    for chunk in range(chunks):
+        for dest in range(length):
+            @pl.when(z == dest)
+            def _():
+                total = part[chunk, dest]
+                if dest > 0:
+                    upward(chunk, dest).wait_recv()
+                    total = total + passing[chunk, dest + 1]
+                if dest < length - 1:
+                    downward(chunk, dest).wait_recv()
+                    total = total + passing[chunk, dest]
+                sums[:, chunk * LANES:(chunk + 1) * LANES] = total
+
+    values = sums[...]
+    part_mean = jnp.mean(values, -1, keepdims=True)
+    apart = values - part_mean
+    spread = jnp.sum(apart * apart, -1, keepdims=True)
+    stats[me, 0:8] = to_row(part_mean)
+    stats[me, 8:16] = to_row(spread)
+    stat_copies = [
+        go(remote(stats.at[me], stats.at[me], stat_send.at[step], stat_recv.at[step], device))
+        for step, device in enumerate(devices)
+    ]
+    for copy in stat_copies:
+        copy.wait_recv()
+    means = [stats[index, 0:1] for index in range(plane.size)]
+    row_mean = sum(means) * (1.0 / plane.size)
+    row_var = sum([stats[index, 8:9] for index in range(plane.size)])
+    for mean in means:
+        row_var = row_var + width * (mean - row_mean) * (mean - row_mean)
+    scale = to_column(lax.rsqrt(row_var * (1.0 / feature_width) + 1e-06))
+    own = pl.ds(pl.multiple_of(me * width, LANES), width)
+    parts[...] = (
+        (values - to_column(row_mean)) * scale * gain[:, own] + shift[:, own]
+    ).astype(jnp.bfloat16)
+    merged_rows = rows // plane.wide
+
+    def rows_of(index):
+        return pl.ds(pl.multiple_of(index // plane.heads * merged_rows, merged_rows), merged_rows)
+
+    norm_copies = [
+        go(remote(parts.at[rows_of(other)], normed.at[:, own], norm_send.at[step],
+                  norm_recv.at[step], devices[step]))
+        for step, other in enumerate(others)
+    ]
+    mine = pltpu.make_async_copy(parts.at[rows_of(me)], normed.at[:, own], own_sem)
+    mine.start()
+    mine.wait()
+    for copy in norm_copies:
+        copy.wait_recv()
+    for copy in started:
+        copy.wait_send()
+    for chunk in range(chunks):
+        for dest in range(length):
+            @pl.when(z < dest)
+            def _():
+                upward(chunk, dest).wait_send()
+
+            @pl.when(z > dest)
+            def _():
+                downward(chunk, dest).wait_send()
+
+
+def front(number, plane, line, tokens, ids, gain, shift):
+    src_rows, feature_width = tokens.shape
+    width = feature_width // plane.size
+    chunks = width // LANES
+    merged_rows = src_rows * plane.heads // RATIO
+    rows = plane.wide * merged_rows
+    dma = pltpu.SemaphoreType.DMA
+    others = plane.size - 1
+    return pl.pallas_call(
+        functools.partial(front_kernel, plane, line, chunks),
+        out_shape=[
+            jax.ShapeDtypeStruct((merged_rows, feature_width), jnp.bfloat16),
+            jax.ShapeDtypeStruct((plane.size, 1, src_rows), jnp.int32),
+        ],
+        in_specs=[VMEM] * 4,
+        out_specs=[VMEM] * 2,
+        scratch_shapes=[
+            pltpu.VMEM((chunks, plane.size, src_rows, LANES), jnp.bfloat16),
+            pltpu.VMEM((chunks, line.size, rows, LANES), jnp.float32),
+            pltpu.VMEM((chunks, line.size + 1, rows, LANES), jnp.float32),
+            pltpu.VMEM((rows, width), jnp.float32),
+            pltpu.VMEM((plane.size, 16, rows), jnp.float32),
+            pltpu.VMEM((rows, width), jnp.bfloat16),
+            dma((others,)),
+            dma((others,)),
+            dma((chunks, others)),
+            dma((chunks, others)),
+            dma((chunks, line.size + 1)),
+            dma((chunks, line.size + 1)),
+            dma((others,)),
+            dma((others,)),
+            dma((others,)),
+            dma((others,)),
+            dma(()),
+        ],
+        compiler_params=pltpu.CompilerParams(
+            collective_id=number, has_side_effects=True, vmem_limit_bytes=56 * 2**20
+        ),
+        name="front",
+    )(tokens, ids, gain, shift)
+
+
+def project_kernel(normed, weights, gains, out):
+    made = jnp.dot(normed[...], weights[0], preferred_element_type=jnp.float32)
+    plain = pl.program_id(0) == 2
+    for start in range(0, made.shape[1], HDIM):
+        one = made[:, start:start + HDIM]
+        scaled = rms_scale(one) * gains[0]
+        out[0, :, start:start + HDIM] = jnp.where(plain, one, scaled).astype(jnp.bfloat16)
+
+
+def project(normed, weights, gains):
+    rows, depth = normed.shape
+    width = weights.shape[2]
+    return pl.pallas_call(
+        project_kernel,
+        grid=(3,),
+        out_shape=jax.ShapeDtypeStruct((3, rows, width), jnp.bfloat16),
+        in_specs=[
+            pl.BlockSpec((rows, depth), lambda j: (0, 0)),
+            pl.BlockSpec((1, depth, width), lambda j: (j, 0, 0)),
+            pl.BlockSpec((1, 1, HDIM), lambda j: (j, 0, 0)),
+        ],
+        out_specs=pl.BlockSpec((1, rows, width), lambda j: (j, 0, 0)),
+        compiler_params=pltpu.CompilerParams(vmem_limit_bytes=56 * 2**20),
+        name="project",
+    )(normed, weights, gains)
+
+
+def attend_kernel(mine, pairs, w_out, out):
+    rows, width = mine.shape[1], mine.shape[2]
+    heads = []
+    for start in range(0, width, HDIM):
+        spot = slice(start, start + HDIM)
+        keys = pairs[:, 0, :, spot].reshape(-1, HDIM)
+        values = pairs[:, 1, :, spot].reshape(-1, HDIM)
+        scores = lax.dot_general(
+            mine[0, :, spot], keys, (((1,), (1,)), ((), ())), preferred_element_type=jnp.float32
+        )
+        expo = jnp.exp(scores - jnp.max(scores, -1, keepdims=True))
+        total = jnp.sum(expo, -1, keepdims=True)
+        weighted = jnp.dot(expo.astype(jnp.bfloat16), values, preferred_element_type=jnp.float32)
+        heads.append((weighted / total).astype(jnp.bfloat16))
+    attended = jnp.concatenate(heads, axis=1)
+    out[...] = jnp.dot(attended, w_out[...], preferred_element_type=jnp.float32).astype(jnp.bfloat16)
+
+
+def attend(made, pairs, w_out):
+    return pl.pallas_call(
+        attend_kernel,
+        out_shape=jax.ShapeDtypeStruct((made.shape[1], w_out.shape[1]), jnp.bfloat16),
+        in_specs=[VMEM] * 3,
+        out_specs=VMEM,
+        compiler_params=pltpu.CompilerParams(vmem_limit_bytes=56 * 2**20),
+        name="attend",
+    )(made, pairs, w_out)
 
 
 def on_device(
@@ -208,88 +465,16 @@
     plane_rows = wide * merged_rows
 
     destination = (owner_shard[:, 0] * merged_rows + dest_slot)[None, :]
-    seen, seen_ids = exchange(
-        0,
-        plane,
-        [tokens, destination],
-        [(plane.size, src_rows, part), (plane.size, 1, src_rows)],
-        [own_columns, whole],
-        [block, block],
-    )
-    seen = seen.reshape(plane_tokens, part)
+    normed, seen_ids = front(0, plane, line, tokens, destination, norm_gain[None], norm_shift[None])
     seen_ids = seen_ids.reshape(plane_tokens)
-    selector = jnp.arange(seq_count * merged_rows, dtype=jnp.int32)[:, None] == seen_ids[None, :]
-    partial_sums = jnp.dot(selector.astype(jnp.bfloat16), seen, preferred_element_type=jnp.float32)
-    [gathered] = exchange(
-        1,
-        line,
-        [partial_sums.reshape(line.size, plane_rows, part)],
-        [(line.size, plane_rows, part)],
-        [block],
-        [block],
-    )
-    sums = jnp.sum(gathered, 0)
-    part_mean = jnp.mean(sums, -1)
-    part_spread = jnp.sum((sums - part_mean[:, None]) ** 2, -1)
-    [stats] = exchange(
-        2,
-        plane,
-        [jnp.stack([part_mean, part_spread])],
-        [(plane.size, 2, plane_rows)],
-        [whole],
-        [block],
-    )
-    row_mean = jnp.mean(stats[:, 0], 0)
-    apart = stats[:, 0] - row_mean[None, :]
-    row_var = (jnp.sum(stats[:, 1], 0) + part * jnp.sum(apart * apart, 0)) / feature_width
 
     def own_part(vector):
         return lax.dynamic_slice(vector, (first_column,), (part,))
 
-    normed = (
-        (sums - row_mean[:, None]) * lax.rsqrt(row_var + 1e-06)[:, None] * own_part(norm_gain)
-        + own_part(norm_shift)
-    ).astype(jnp.bfloat16)
-    [normed] = exchange(
-        3,
-        plane,
-        [normed.reshape(wide, merged_rows, part)],
-        [(merged_rows, feature_width)],
-        [lambda ref, index: ref.at[index // head_count]],
-        [own_columns],
-    )
-    head_width = w_qkv.shape[2]
-    local_heads = head_width // HDIM
-    weights = jnp.transpose(w_qkv, (1, 0, 2))
-
-    def projected(which):
-        return jnp.dot(normed, weights[which], preferred_element_type=jnp.float32)
-
-    def by_head(values_in):
-        return values_in.reshape(merged_rows, local_heads, HDIM)
-
-    queries = (rms_scale(by_head(projected(0))) * query_gain / math.sqrt(HDIM)).astype(jnp.bfloat16)
-    keys_local = (rms_scale(by_head(projected(1))) * key_gain).astype(jnp.bfloat16)
-    values_local = projected(2).astype(jnp.bfloat16)
-    keys_all, values_all = gather_seq(
-        4,
-        seq_count,
-        [keys_local.reshape(merged_rows, head_width), values_local],
-    )
-    keys_all = keys_all.reshape(-1, local_heads, HDIM)
-    values_all = values_all.reshape(-1, local_heads, HDIM)
-    scores = jnp.einsum("qhd,khd->hqk", queries, keys_all, preferred_element_type=jnp.float32)
-    expweights = jnp.exp(scores - jnp.max(scores, -1, keepdims=True))
-    total = jnp.sum(expweights, -1)
-    weighted = jnp.einsum(
-        "hqk,khd->qhd",
-        expweights.astype(jnp.bfloat16),
-        values_all,
-        preferred_element_type=jnp.float32,
-    )
-    attended = (weighted / jnp.transpose(total)[:, :, None]).astype(jnp.bfloat16)
-    attended = attended.reshape(merged_rows, head_width)
-    partial_out = jnp.dot(attended, w_out, preferred_element_type=jnp.float32).astype(jnp.bfloat16)
+    gains = jnp.stack([query_gain / math.sqrt(HDIM), key_gain, jnp.ones_like(key_gain)])
+    made = project(normed, jnp.transpose(w_qkv, (1, 0, 2)), gains[:, None])
+    [pairs] = gather_seq(4, seq_count, [made])
+    partial_out = attend(made, pairs, w_out)
     [pieces] = exchange(
         5,
         plane,

time: 200 us -> 164 us (0.82)
  local copies, waits for them, and re-layouts: 27.4 us -> 3.48 us
  matrix products: 22.5 us -> 3.31 us
  Pallas kernels: 142 us -> 152 us
  other arithmetic: 6.68 us -> 4.55 us
    pallas_call x0 -> x3, Pallas kernels: none -> 72.2 us  [the longest x1 61.8 us: front(): pl.pallas_call(functools.partial(front_kernel, plane, line, chunks), out_...]
    pallas_call x7 -> x3, Pallas kernels: 113 us -> 45 us  [exchange(): pl.pallas_call(functools.partial(exchange_kernel, group, count, source_of...]
    dot_general x7 -> x0, matrix products: 17.5 us -> none  [the longest x3 8.17 us: projected(): return jnp.dot(normed, weights[which], preferred_element_type=jnp.float32)]
    dot_general x3 -> x0, local copies, waits for them, and re-layouts: 13.7 us -> none  [projected(): return jnp.dot(normed, weights[which], preferred_element_type=jnp.float32)]
    reshape x3 -> x0, local copies, waits for them, and re-layouts: 6.17 us -> none  [the longest x1 3.26 us: on_device(): keys_all = keys_all.reshape(-1, local_heads, HDIM)]
    pallas_call x1, Pallas kernels: 29.8 us -> 34.4 us  [gather_seq(): pl.pallas_call(functools.partial(gather_kernel, wide, length, count), out...]
    reduce_sum x4 -> x0, other arithmetic: 2.65 us -> none  [the longest x1 1.61 us: on_device(): part_mean = jnp.mean(sums, -1)]
    pallas_call x1 -> x0, local copies, waits for them, and re-layouts: 2.45 us -> none  [gather_seq(): pl.pallas_call(functools.partial(gather_kernel, wide, length, count), out...]
where the time goes in v2:
time: 164 us; the launch traced here: 163 us
  Pallas kernels  152 us (93%)
  other arithmetic  4.55 us (3%)
  local copies, waits for them, and re-layouts  3.48 us (2%)
  matrix products  3.31 us (2%)
    pallas_call x1, Pallas kernels, front(): pl.pallas_call(functools.partial(front_kernel, plane, line, chunks), out_...  61.8 us
    pallas_call x3, Pallas kernels, exchange(): pl.pallas_call(functools.partial(exchange_kernel, group, count, source_of...  45 us
    pallas_call x1, Pallas kernels, gather_seq(): pl.pallas_call(functools.partial(gather_kernel, wide, length, count), out...  34.4 us
    pallas_call x1, Pallas kernels, project(): pl.pallas_call(project_kernel, grid=(3,), out_shape=jax.ShapeDtypeStruct(...  5.59 us
    pallas_call x1, Pallas kernels, attend(): pl.pallas_call(attend_kernel, out_shape=jax.ShapeDtypeStruct((made.shape[...  4.79 us
    dot_general x1, matrix products, on_device(): jnp.dot(chooser.astype(jnp.bfloat16), merged_all, preferred_element_type=...  3.31 us

profile of v2, /device:TPU:25, one launch (start us, length us, event | category | flops | bytes accessed | tf_op | source)
XLA Modules:
  0.0 163.0 jit_solution(11329556898318212655)
XLA Ops:
  0.0 1.2 fusion.4.ids
  1.2 61.8 %front.1 = (bf16[128,3072]{1,0:T(8,128)(2,1)}, s32[8,1,128]{2,1,0:T(1,128)}) custom-call(bf16[128,3072]{1,0:T(8,128)(2,1)} %tokens.1, s32[1,128]{1,0:T(1,128)} %fusion.4.ids, f32[1,3072]{1,0:T(1,128)} %bitcast.27, f32[1,3072]{1,0:T(1,128)} %bitcast.28), custom_call_target="tpu_custom_call" | custom-call | tf_op jit(solution)/shard_map/front/pallas_call | solution.py:353
  63.0 0.7 multiply_bitcast_fusion
  63.7 0.1 pad.2.clone
  63.8 0.7 maximum_maximum_fusion
  64.5 0.6 broadcast_in_dim.17.gains
  65.1 5.6 %project.1.refs_0_.mine = bf16[3,128,384]{2,1,0:T(8,128)(2,1)} custom-call(bf16[128,3072]{1,0:T(8,128)(2,1)} %get-tuple-element.8.normed, bf16[3,3072,384]{2,1,0:T(8,128)(2,1)} %bitcast.24, f32[3,1,128]{2,1,0:T(1,128)} %broadcast_in_dim.17.gains), custom_call_target="tpu_custom_call" | custom-call | tf_op jit(solution)/shard_map/project/pallas_call | solution.py:399
  70.6 34.4 %gather_4.1.pairs = bf16[8,2,128,384]{3,2,1,0:T(8,128)(2,1)} custom-call(bf16[3,128,384]{2,1,0:T(8,128)(2,1)} %project.1.refs_0_.mine), custom_call_target="tpu_custom_call" | custom-call | tf_op jit(solution)/shard_map/gather_4/pallas_call | solution.py:166
  105.1 4.8 %attend.1.refs_0_ = bf16[128,3072]{1,0:T(8,128)(2,1)} custom-call(bf16[3,128,384]{2,1,0:T(8,128)(2,1)} %project.1.refs_0_.mine, bf16[8,2,128,384]{3,2,1,0:T(8,128)(2,1)} %gather_4.1.pairs, bf16[384,3072]{1,0:T(8,128)(2,1)} %w_out.1), custom_call_target="tpu_custom_call" | custom-call | tf_op jit(solution)/shard_map/attend/pallas_call | solution.py:433
  109.8 0.0 copy-start
  109.9 12.6 %exchange_5.1 = bf16[8,128,384]{2,1,0:T(8,128)(2,1)} custom-call(bf16[128,3072]{1,0:T(8,128)(2,1)} %attend.1.refs_0_), custom_call_target="tpu_custom_call" | custom-call | tf_op jit(solution)/shard_map/exchange_5/pallas_call | solution.py:89
  122.4 1.3 convert_reduce_fusion
  123.7 0.8 dynamic_slice.3
  124.5 0.7 fusion.3.refs_0_
  125.2 20.4 %exchange_6.1 = bf16[4,256,384]{2,1,0:T(8,128)(2,1)} custom-call(bf16[256,384]{1,0:T(8,128)(2,1)} %fusion.3.refs_0_), custom_call_target="tpu_custom_call" | custom-call | tf_op jit(solution)/shard_map/exchange_6/pallas_call | solution.py:89
  145.6 0.0 copy-done
  145.6 3.3 %fusion.2 = bf16[1024,384]{1,0:T(8,128)(2,1)} fusion(bf16[1024,384]{1,0:T(8,128)(2,1)} %bitcast.26, s32[1024]{0:T(1024)S(1)} %bitcast.30), kind=kOutput, calls=%fused_computation.4 | convolution fusion | flops 806748160 | bytes 1576960 | tf_op jit(solution)/shard_map/dot_general | solution.py:498
  148.9 12.0 %exchange_7.1 = bf16[128,3072]{1,0:T(8,128)(2,1)} custom-call(bf16[8,128,384]{2,1,0:T(8,128)(2,1)} %bitcast.25), custom_call_target="tpu_custom_call" | custom-call | tf_op jit(solution)/shard_map/exchange_7/pallas_call | solution.py:89
  161.0 2.1 %copy.12 = bf16[128,3072]{1,0:T(8,128)(2,1)} copy(bf16[128,3072]{1,0:T(8,128)(2,1)} %exchange_7.1) | data formatting | bytes 1572864
Async XLA Ops:
  109.8 35.8 %copy-start = (s32[8,1,128]{2,1,0:T(1,128)S(1)}, s32[8,1,128]{2,1,0:T(1,128)}, u32[]{:S(2)}) copy-start(s32[8,1,128]{2,1,0:T(1,128)} %get-tuple-element.7) | copy-start | bytes 12292

commit v3 on v2

--- a/solution.py
+++ b/solution.py
@@ -53,66 +53,6 @@
     for device in devices:
         pl.semaphore_signal(barrier, inc=1, device_id=device, device_id_type=MESH)
     pl.semaphore_wait(barrier, len(devices))
-
-
-def exchange_kernel(group, count, source_of, target_of, *refs):
-    sources, targets = refs[:count], refs[count : 2 * count]
-    send_sem, recv_sem, own_sem = refs[2 * count :]
-    size, me = group.size, group.me()
-    others = [lax.rem(me + step, size) for step in range(1, size)]
-    greet([group.device(other) for other in others])
-    copies = []
-    for step, other in enumerate(others):
-        for item in range(count):
-            copy = pltpu.make_async_remote_copy(
-                src_ref=source_of[item](sources[item], other),
-                dst_ref=target_of[item](targets[item], me),
-                send_sem=send_sem.at[item, step],
-                recv_sem=recv_sem.at[item, step],
-                device_id=group.device(other),
-                device_id_type=MESH,
-            )
-            copy.start()
-            copies.append(copy)
-    for item in range(count):
-        own = pltpu.make_async_copy(
-            source_of[item](sources[item], me), target_of[item](targets[item], me), own_sem.at[item]
-        )
-        own.start()
-        copies.append(own)
-    for copy in copies:
-        copy.wait()
-
-
-def exchange(number, group, arrays, shapes, source_of, target_of):
-    count = len(arrays)
-    return pl.pallas_call(
-        functools.partial(exchange_kernel, group, count, source_of, target_of),
-        out_shape=[
-            jax.ShapeDtypeStruct(shape, array.dtype) for shape, array in zip(shapes, arrays)
-        ],
-        in_specs=[ANY] * count,
-        out_specs=[ANY] * count,
-        scratch_shapes=[
-            pltpu.SemaphoreType.DMA((count, group.size - 1)),
-            pltpu.SemaphoreType.DMA((count, group.size - 1)),
-            pltpu.SemaphoreType.DMA((count,)),
-        ],
-        compiler_params=pltpu.CompilerParams(collective_id=number, has_side_effects=True),
-        name="exchange_" + str(number),
-    )(*arrays)
-
-
-def whole(ref, index):
-    return ref
-
-
-def block(ref, index):
-    return ref.at[index]
-
-
-def columns(width, ref, index):
-    return ref.at[:, pl.ds(pl.multiple_of(index * width, width), width)]
 
 
 def gather_kernel(wide, length, count, *refs):
@@ -411,7 +351,7 @@
     )(normed, weights, gains)
 
 
-def attend_kernel(mine, pairs, w_out, out):
+def attend_kernel(mine, pairs, w_out, partial):
     rows, width = mine.shape[1], mine.shape[2]
     heads = []
     for start in range(0, width, HDIM):
@@ -426,18 +366,172 @@
         weighted = jnp.dot(expo.astype(jnp.bfloat16), values, preferred_element_type=jnp.float32)
         heads.append((weighted / total).astype(jnp.bfloat16))
     attended = jnp.concatenate(heads, axis=1)
-    out[...] = jnp.dot(attended, w_out[...], preferred_element_type=jnp.float32).astype(jnp.bfloat16)
-
-
-def attend(made, pairs, w_out):
+    partial[...] = jnp.dot(
+        attended, w_out[...], preferred_element_type=jnp.float32
+    ).astype(jnp.bfloat16)
+
+
+def tail_kernel(
+    plane, line, chunks, mine, pairs, w_out, gate, ids, out, partial, pieces, merged, chooser,
+    fetched, piece_send, piece_recv, up_send, up_recv, down_send, down_recv, back_send, back_recv,
+):
+    me, z, length = plane.me(), line.me(), line.size
+    src_rows = out.shape[0]
+    rows = merged.shape[2]
+    merged_rows = rows // plane.wide
+    width = chunks * LANES
+    others = [lax.rem(me + step, plane.size) for step in range(1, plane.size)]
+    devices = [plane.device(other) for other in others]
+    above, below = lax.rem(z + 1, length), lax.rem(z + length - 1, length)
+    along = [lax.rem(z + step, length) for step in range(1, length)]
+    greet(devices + [line.device(other) for other in along])
+
+    def slab(index, chunk):
+        return pl.ds(pl.multiple_of(index * width + chunk * LANES, LANES), LANES)
+
+    attend_kernel(mine, pairs, w_out, partial)
+    started = []
+
+    def go(copy):
+        copy.start()
+        started.append(copy)
+        return copy
+
+    piece_copies = [
+        [
+            go(remote(partial.at[:, slab(other, chunk)], pieces.at[chunk, me],
+                      piece_send.at[chunk, step], piece_recv.at[chunk, step], devices[step]))
+            for step, other in enumerate(others)
+        ]
+        for chunk in range(chunks)
+    ]
+    for chunk in range(chunks):
+        pieces[chunk, me] = partial[:, slab(me, chunk)]
+    places = lax.broadcasted_iota(jnp.int32, (1, length * rows), 1)
+    for index in range(plane.size):
+        chooser[index * src_rows:(index + 1) * src_rows] = (
+            (to_column(ids[index]) == places).astype(jnp.float32).astype(jnp.bfloat16)
+        )
+
+    def upward(chunk, far):
+        spot = merged.at[chunk, z - far]
+        return remote(spot, spot, up_send.at[chunk, far], up_recv.at[chunk, far], line.device(above))
+
+    def downward(chunk, far):
+        spot = merged.at[chunk, z + far]
+        return remote(spot, spot, down_send.at[chunk, far], down_recv.at[chunk, far],
+                      line.device(below))
+
+    def came_up(chunk, far):
+        spot = merged.at[chunk, z - far]
+        return remote(spot, spot, up_send.at[chunk, far - 1], up_recv.at[chunk, far - 1],
+                      line.device(above))
+
+    def came_down(chunk, far):
+        spot = merged.at[chunk, z + far]
+        return remote(spot, spot, down_send.at[chunk, far - 1], down_recv.at[chunk, far - 1],
+                      line.device(below))
+
+    def pass_on(chunk, far):
+        if far < length - 1:
+            @pl.when((z >= far) & (z < length - 1))
+            def _():
+                upward(chunk, far).start()
+
+            @pl.when((z + far < length) & (z > 0))
+            def _():
+                downward(chunk, far).start()
+
+    for turn in range(chunks + length - 1):
+        for far in range(length):
+            chunk = turn - far
+            if not 0 <= chunk < chunks:
+                continue
+            if far == 0:
+                for copy in piece_copies[chunk]:
+                    copy.wait_recv()
+                for y in range(plane.wide):
+                    total = sum(
+                        [
+                            pieces[chunk, y * plane.heads + head].astype(jnp.float32)
+                            for head in range(plane.heads)
+                        ]
+                    )
+                    merged[chunk, z, y * merged_rows:(y + 1) * merged_rows] = (
+                        total * gate[:, slab(me, chunk)]
+                    ).astype(jnp.bfloat16)
+            else:
+                @pl.when(z >= far)
+                def _():
+                    came_up(chunk, far).wait_recv()
+
+                @pl.when(z + far < length)
+                def _():
+                    came_down(chunk, far).wait_recv()
+            pass_on(chunk, far)
+            if far == length - 1:
+                fetched[chunk] = (
+                    jnp.dot(
+                        chooser[...],
+                        merged[chunk].reshape(length * rows, LANES),
+                        preferred_element_type=jnp.float32,
+                    )
+                    .astype(jnp.bfloat16)
+                    .reshape(plane.size, src_rows, LANES)
+                )
+                for step, other in enumerate(others):
+                    go(remote(fetched.at[chunk, other], out.at[:, slab(me, chunk)],
+                              back_send.at[chunk, step], back_recv.at[chunk, step], devices[step]))
+                out[:, slab(me, chunk)] = fetched[chunk, me]
+    for chunk in range(chunks):
+        for far in range(length - 1):
+            @pl.when((z >= far) & (z < length - 1))
+            def _():
+                upward(chunk, far).wait_send()
+
+            @pl.when((z + far < length) & (z > 0))
+            def _():
+                downward(chunk, far).wait_send()
+    backs = started[len(others) * chunks:]
+    for copy in backs:
+        copy.wait_recv()
+    for copy in started:
+        copy.wait_send()
+
+
+def tail(number, plane, line, made, pairs, w_out, gate, ids):
+    src_rows, feature_width = ids.shape[2], w_out.shape[1]
+    merged_rows = made.shape[1]
+    width = feature_width // plane.size
+    chunks = width // LANES
+    rows = plane.wide * merged_rows
+    dma = pltpu.SemaphoreType.DMA
+    others = plane.size - 1
     return pl.pallas_call(
-        attend_kernel,
-        out_shape=jax.ShapeDtypeStruct((made.shape[1], w_out.shape[1]), jnp.bfloat16),
-        in_specs=[VMEM] * 3,
+        functools.partial(tail_kernel, plane, line, chunks),
+        out_shape=jax.ShapeDtypeStruct((src_rows, feature_width), jnp.bfloat16),
+        in_specs=[VMEM] * 5,
         out_specs=VMEM,
-        compiler_params=pltpu.CompilerParams(vmem_limit_bytes=56 * 2**20),
-        name="attend",
-    )(made, pairs, w_out)
+        scratch_shapes=[
+            pltpu.VMEM((merged_rows, feature_width), jnp.bfloat16),
+            pltpu.VMEM((chunks, plane.size, merged_rows, LANES), jnp.bfloat16),
+            pltpu.VMEM((chunks, line.size, rows, LANES), jnp.bfloat16),
+            pltpu.VMEM((plane.size * src_rows, line.size * rows), jnp.bfloat16),
+            pltpu.VMEM((chunks, plane.size, src_rows, LANES), jnp.bfloat16),
+            dma((chunks, others)),
+            dma((chunks, others)),
+            dma((chunks, line.size)),
+            dma((chunks, line.size)),
+            dma((chunks, line.size)),
+            dma((chunks, line.size)),
+            dma((chunks, others)),
+            dma((chunks, others)),
+        ],
+        compiler_params=pltpu.CompilerParams(
+            collective_id=number, has_side_effects=True, vmem_limit_bytes=56 * 2**20
+        ),
+        name="tail",
+    )(made, pairs, w_out, gate, ids)
 
 
 def on_device(
@@ -457,56 +551,12 @@
     src_rows, feature_width = tokens.shape
     merged_rows = src_rows * head_count // RATIO
     plane, line = Plane(seq_count, head_count), Line(seq_count, head_count)
-    wide = plane.wide
-    part = feature_width // plane.size
-    own_columns = functools.partial(columns, part)
-    first_column = plane.me() * part
-    plane_tokens = plane.size * src_rows
-    plane_rows = wide * merged_rows
-
     destination = (owner_shard[:, 0] * merged_rows + dest_slot)[None, :]
     normed, seen_ids = front(0, plane, line, tokens, destination, norm_gain[None], norm_shift[None])
-    seen_ids = seen_ids.reshape(plane_tokens)
-
-    def own_part(vector):
-        return lax.dynamic_slice(vector, (first_column,), (part,))
-
     gains = jnp.stack([query_gain / math.sqrt(HDIM), key_gain, jnp.ones_like(key_gain)])
     made = project(normed, jnp.transpose(w_qkv, (1, 0, 2)), gains[:, None])
     [pairs] = gather_seq(4, seq_count, [made])
-    partial_out = attend(made, pairs, w_out)
-    [pieces] = exchange(
-        5,
-        plane,
-        [partial_out],
-        [(plane.size, merged_rows, part)],
-        [own_columns],
-        [block],
-    )
-    pieces = pieces.reshape(wide, head_count, merged_rows, part).astype(jnp.float32)
-    merged_out = (jnp.sum(pieces, 1) * own_part(out_gate)).astype(jnp.bfloat16)
-    [merged_all] = exchange(
-        6,
-        line,
-        [merged_out.reshape(plane_rows, part)],
-        [(line.size, plane_rows, part)],
-        [whole],
-        [block],
-    )
-    merged_all = merged_all.reshape(seq_count * merged_rows, part)
-    chooser = seen_ids[:, None] == jnp.arange(seq_count * merged_rows, dtype=jnp.int32)[None, :]
-    fetched = jnp.dot(
-        chooser.astype(jnp.bfloat16), merged_all, preferred_element_type=jnp.float32
-    ).astype(jnp.bfloat16)
-    [returned] = exchange(
-        7,
-        plane,
-        [fetched.reshape(plane.size, src_rows, part)],
-        [(src_rows, feature_width)],
-        [block],
-        [own_columns],
-    )
-    return returned
+    return tail(5, plane, line, made, pairs, w_out, out_gate[None], seen_ids)
 
 
 def solution(mesh):

time: 164 us -> 147 us (0.90)
  the two profiles are of different devices: /device:TPU:25 before, /device:TPU:0 now
where the time goes in v3:
time: 147 us; the launch traced here: 146 us
  Pallas kernels  141 us (96%)
  local copies, waits for them, and re-layouts  2.73 us (2%)
  other arithmetic  2.57 us (2%)
    pallas_call x1, Pallas kernels, front(): pl.pallas_call(functools.partial(front_kernel, plane, line, chunks), out_...  67.4 us
    pallas_call x1, Pallas kernels, tail(): pl.pallas_call(functools.partial(tail_kernel, plane, line, chunks), out_s...  39.3 us
    pallas_call x1, Pallas kernels, gather_seq(): pl.pallas_call(functools.partial(gather_kernel, wide, length, count), out...  28.8 us
    pallas_call x1, Pallas kernels, project(): pl.pallas_call(project_kernel, grid=(3,), out_shape=jax.ShapeDtypeStruct(...  5.59 us

profile of v3, /device:TPU:0, one launch (start us, length us, event | category | flops | bytes accessed | tf_op | source)
XLA Modules:
  0.0 146.4 jit_solution(7670260211990512597)
XLA Ops:
  0.0 1.2 fusion.ids
  1.2 0.7 multiply_bitcast_fusion
  1.8 0.1 pad.2.clone
  1.9 0.7 maximum_maximum_fusion
  2.6 0.6 broadcast_in_dim.18.gains
  3.2 67.4 %front.1 = (bf16[128,3072]{1,0:T(8,128)(2,1)}, s32[8,1,128]{2,1,0:T(1,128)}) custom-call(bf16[128,3072]{1,0:T(8,128)(2,1)} %tokens.1, s32[1,128]{1,0:T(1,128)} %fusion.ids, f32[1,3072]{1,0:T(1,128)} %bitcast.16, f32[1,3072]{1,0:T(1,128)} %bitcast.17), custom_call_target="tpu_custom_call" | custom-call | tf_op jit(solution)/shard_map/front/pallas_call | solution.py:293
  70.7 5.6 %project.1.refs_0_.mine = bf16[3,128,384]{2,1,0:T(8,128)(2,1)} custom-call(bf16[128,3072]{1,0:T(8,128)(2,1)} %get-tuple-element.7.normed, bf16[3,3072,384]{2,1,0:T(8,128)(2,1)} %bitcast.14, f32[3,1,128]{2,1,0:T(1,128)} %broadcast_in_dim.18.gains), custom_call_target="tpu_custom_call" | custom-call | tf_op jit(solution)/shard_map/project/pallas_call | solution.py:339
  76.2 28.8 %gather_4.1.pairs = bf16[8,2,128,384]{3,2,1,0:T(8,128)(2,1)} custom-call(bf16[3,128,384]{2,1,0:T(8,128)(2,1)} %project.1.refs_0_.mine), custom_call_target="tpu_custom_call" | custom-call | tf_op jit(solution)/shard_map/gather_4/pallas_call | solution.py:106
  105.0 39.3 %tail.1 = bf16[128,3072]{1,0:T(8,128)(2,1)} custom-call(bf16[3,128,384]{2,1,0:T(8,128)(2,1)} %project.1.refs_0_.mine, bf16[8,2,128,384]{3,2,1,0:T(8,128)(2,1)} %gather_4.1.pairs, bf16[384,3072]{1,0:T(8,128)(2,1)} %w_out.1, f32[1,3072]{1,0:T(1,128)} %bitcast.15, s32[8,1,128]{2,1,0:T(1,128)} %get-tuple-element.8.ids), custom_call_target="tpu_custom_call" | custom-call | tf_op jit(solution)/shard_map/tail/pallas_call | solution.py:510
  144.4 2.1 %copy.12 = bf16[128,3072]{1,0:T(8,128)(2,1)} copy(bf16[128,3072]{1,0:T(8,128)(2,1)} %tail.1) | data formatting | bytes 1572864
